TPU v7x, 32 devices: a whole 2x2x4 slice. The times are simulated.
32 devices in a mesh: dp: 4 (over x, core), shard: 8 (over z, y).
Axes of the slice: x: 2, y: 2, z: 4, core: 2. Of those that a mesh axis runs over, the one named last changes fastest.
Arguments:
- table: float32 [16384, 128], P('shard'), may hold values from -6 to 6
- cross_weight: bfloat16 [1024, 1024], replicated, may hold values from -0.1875 to 0.1875
- cross_bias: float32 [1024], replicated, may hold values from -3 to 3
- top_weight: bfloat16 [1024, 512], replicated, may hold values from -0.1875 to 0.1875
- top_bias: float32 [512], replicated, may hold values from -3 to 3
- out_weight: float32 [512], replicated, may hold values from -0.25 to 0.25
- wanted: int32 [32, 8, 128], P(('dp', 'shard')), may hold values from 0 to 2047, as said below
- slots: int32 [16384, 8, 4], P(('dp', 'shard')), may hold values from 0 to 1023
- lengths: int32 [16384, 8], P(('dp', 'shard')), may hold values from 1 to 4
- logit_grad: float32 [16384], P(('dp', 'shard')), may hold values from -6 to 6
Outputs:
- logits: float32 [16384], P(('dp', 'shard'))
- grad_cross: float32 [1024, 1024], replicated
- grad_top: float32 [1024, 512], replicated
- grad_cross_bias: float32 [1024], replicated
- grad_top_bias: float32 [512], replicated
- grad_out: float32 [512], replicated
- table_grad: float32 [16384, 128], P('shard')
Inputs may be any that keep to these rules, and one draw needn't show every extreme that they name: `wanted`: the 128 rows that one device fetches from one owner are distinct.
All inputs are finite; a program needn't handle non-finite values.
Results may differ from a plain program's by a relative error of at most 0.0084.
Values sent between devices are 32-bit elements; how exact they have to be, the bound alone decides.
No kernel may reach another device: no remote copies, remote signals or barrier semaphores. Data moves between devices by JAX's collectives and lax.ppermute only.
A program may use at most 128 MiB of HBM per device.

v0:
```python
import jax
import jax.numpy as jnp
from jax import lax
from jax.sharding import PartitionSpec as P


def on_device(
    table,
    cross_weight,
    cross_bias,
    top_weight,
    top_bias,
    out_weight,
    wanted,
    slots,
    lengths,
    logit_grad,
):
    emb = table.shape[1]
    samples = slots.shape[0]
    feats = slots.shape[1]
    bag = slots.shape[2]
    requests = wanted[0]
    served = lax.all_to_all(requests, "shard", split_axis=0, concat_axis=0, tiled=True)
    cache = lax.all_to_all(
        jnp.take(table, served, axis=0), "shard", split_axis=0, concat_axis=0, tiled=True
    )
    cache_flat = cache.reshape(-1, emb)
    live = (jnp.arange(bag, dtype=jnp.int32)[None, None, :] < lengths[:, :, None]).astype(
        jnp.float32
    )
    gathered = cache_flat[slots]
    pooled = jnp.sum(gathered * live[..., None], axis=2)
    x0 = pooled.reshape(samples, feats * emb).astype(jnp.bfloat16)
    xfull = x0.astype(jnp.float32)
    yval = jnp.dot(x0, cross_weight, preferred_element_type=jnp.float32) + cross_bias
    hidden = (xfull * yval + xfull).astype(jnp.bfloat16)
    zval = jnp.dot(hidden, top_weight, preferred_element_type=jnp.float32) + top_bias
    sig = jax.nn.sigmoid(zval)
    uval = zval * sig
    logits = jnp.dot(uval, out_weight, precision=lax.Precision.HIGHEST)
    g_out = jnp.dot(logit_grad, uval, precision=lax.Precision.HIGHEST)
    dz = logit_grad[:, None] * out_weight[None, :] * (sig * (1.0 + zval * (1.0 - sig)))
    dzb = dz.astype(jnp.bfloat16)
    g_top = jnp.dot(hidden.T, dzb, preferred_element_type=jnp.float32)
    g_tbias = jnp.sum(dz, axis=0)
    dh = jnp.dot(dzb, top_weight.T, preferred_element_type=jnp.float32)
    dy = dh * xfull
    dyb = dy.astype(jnp.bfloat16)
    g_cross = jnp.dot(x0.T, dyb, preferred_element_type=jnp.float32)
    g_cbias = jnp.sum(dy, axis=0)
    dx = dh * (yval + 1.0) + jnp.dot(dyb, cross_weight.T, preferred_element_type=jnp.float32)
    contrib = dx.reshape(samples, feats, 1, emb) * live[..., None]
    slot_grads = (
        jnp.zeros(cache_flat.shape, jnp.float32).at[slots.reshape(-1)].add(contrib.reshape(-1, emb))
    )
    returned = lax.all_to_all(
        slot_grads.reshape(cache.shape), "shard", split_axis=0, concat_axis=0, tiled=True
    )
    every_ids, every_grads = (
        lax.all_gather(served, "dp", axis=0, tiled=True),
        lax.all_gather(returned, "dp", axis=0, tiled=True),
    )
    table_grad = (
        jnp.zeros(table.shape, jnp.float32)
        .at[every_ids.reshape(-1)]
        .add(every_grads.reshape(-1, emb))
    )
    summed = lax.psum((g_cross, g_top, g_cbias, g_tbias, g_out), ("dp", "shard"))
    return (logits, summed[0], summed[1], summed[2], summed[3], summed[4], table_grad)


def solution(mesh):
    placed = (
        P("shard", None),
        P(),
        P(),
        P(),
        P(),
        P(),
        P(("dp", "shard"), None, None),
        P(("dp", "shard"), None, None),
        P(("dp", "shard"), None),
        P(("dp", "shard")),
    )
    return jax.shard_map(
        on_device,
        mesh=mesh,
        in_specs=placed,
        out_specs=(P(("dp", "shard")), P(), P(), P(), P(), P(), P("shard", None)),
        check_vma=False,
    )
```

profile of v0, /device:TPU:0, one launch (start us, length us, event | category | flops | bytes accessed | tf_op | source)
XLA Modules:
  0.0 422.9 jit_solution(4629583356204810095)
XLA Ops:
  8.0 0.0 copy-start
  8.0 7.5 %all-to-all-start = ((s32[8,1,128]{2,1,0:T(1,128)}), s32[8,1,128]{2,1,0:T(1,128)S(1)}, u32[]{:S(2)}, u32[]{:S(2)}) async-start(s32[8,1,128]{2,1,0:T(1,128)} %bitcast.62), calls=%async_computation | async-start | bytes 8192 | tf_op jit(solution)/shard_map/all_to_all | solution.py:24
  15.5 0.0 copy-start.6
  15.5 0.0 copy-start.1
  15.5 2.9 copy.26
  18.4 3.3 reshape.146
  21.7 0.1 compare_select_fusion
  21.8 0.0 copy-done.6
  21.8 0.1 copy.25
  21.9 0.0 all-to-all-done
  21.9 0.0 copy-done.1
  21.9 4.0 gather_fusion
  26.0 2.0 broadcast_select_fusion
  28.0 6.0 %all-to-all-start.1 = ((f32[8,128,128]{2,1,0:T(8,128)}), f32[8,128,128]{2,1,0:T(8,128)S(1)}, u32[]{:S(2)}, u32[]{:S(2)}) async-start(f32[8,128,128]{2,1,0:T(8,128)} %broadcast_select_fusion), calls=%async_computation.1 | async-start | bytes 1048576 | tf_op jit(solution)/shard_map/all_to_all | solution.py:25
  34.0 0.2 all-gather.3.cloned.1.call-start
  34.2 2.6 fusion.4
  36.8 3.2 reshape.149
  40.0 0.0 copy-done.5
  40.1 2.0 copy.24
  42.0 3.2 reshape.160
  45.3 2.7 all-to-all-done.1
  48.0 54.8 %gather_fusion.1 = f32[16384,128]{1,0:T(8,128)} fusion(f32[1024,128]{1,0:T(8,128)S(1)} %bitcast.48, s32[16384]{0:T(1024)S(1)} %broadcast_clamp_fusion), kind=kCustom, calls=%fused_computation.1 | custom fusion | bytes 16842752 | tf_op jit(solution)/shard_map/gather | solution.py:32
  102.7 7.9 %multiply_reduce_fusion = bf16[512,8,128]{2,1,0:T(8,128)(2,1)S(1)} fusion(f32[512,8,4,128]{3,2,1,0:T(4,128)} %bitcast.49, f32[512,8,4]{2,1,0:T(8,128)} %fusion.4), kind=kLoop, calls=%fused_computation.6 | loop fusion | flops 3670016 | bytes 9502720 | tf_op jit(solution)/shard_map/reduce_sum | solution.py:33
  110.6 0.0 copy-done
  110.6 0.0 copy-done.8
  110.6 0.0 copy-start.7
  110.6 0.0 copy-start.9
  110.6 0.0 copy-start.10
  110.7 0.0 copy-start.11
  110.7 1.4 fusion.3
  112.0 0.0 copy-start.14
  112.0 0.0 copy-done.7
  112.1 0.0 copy-done.9
  112.1 0.0 copy-done.10
  112.1 0.0 copy-done.11
  112.1 1.0 fusion.33
  113.1 0.0 copy-done.14
  113.1 0.0 copy-start.12
  113.1 1.1 fusion.5
  114.2 0.0 copy-done.12
  114.2 0.0 copy-start.2
  114.2 1.3 add_bitcast_fusion
  115.5 0.0 copy-done.2
  115.5 1.8 copy.28
  117.3 7.3 %mul.73 = f32[512,8,4,128]{3,2,1,0:T(4,128)} broadcast(f32[512,8,128]{2,1,0:T(8,128)} %bitcast.55), dimensions={0,1,3} | broadcast | bytes 10485760 | tf_op jit(solution)/shard_map/mul | solution.py:53
  124.7 97.1 %scatter_custom_fusion = f32[1024,128]{1,0:T(8,128)} fusion(s32[16384]{0:T(1024)S(1)} %bitcast.60, f32[16384,128]{1,0:T(8,128)} %bitcast.50, f32[16384]{0:T(1024)S(1)} %reshape.149, f32[]{:T(128)} %constant.12.clone.1), kind=kCustom, calls=%fused_computation.4 | custom fusion | flops 4194304 | bytes 8978436 | tf_op jit(solution)/shard_map/scatter-add | solution.py:55
  221.7 18.0 %all_to_all.25 = f32[8,128,128]{2,1,0:T(8,128)} all-to-all(f32[8,128,128]{2,1,0:T(8,128)} %bitcast.56), channel_id=1, replica_groups=mesh['dp'=4,'shard'=8] {'shard'}, dimensions={0} | all-to-all | bytes 1048576 | tf_op jit(solution)/shard_map/all_to_all | solution.py:57
  239.7 0.0 all-gather.3.cloned.1.call-update
  239.8 0.0 all-reduce.4.cloned.1.call-start
  239.8 0.0 copy-start.3
  239.8 4.0 fusion.21
  243.8 0.0 copy-done.3
  243.8 3.3 fusion.8
  247.2 0.0 all-reduce.4.cloned.1.call-update
  247.2 5.5 %all-gather = s32[32,1,128]{2,1,0:T(1,128)S(1)} all-gather(s32[8,1,128]{2,1,0:T(1,128)S(1)} %all-to-all-done), channel_id=2, replica_groups=mesh['dp'=4,'shard'=8] {'dp'}, dimensions={0}, use_global_device_ids=true | all-gather | bytes 20480 | tf_op jit(solution)/shard_map/all_gather | solution.py:61
  252.7 0.0 copy-done.13
  252.7 0.9 fusion.25
  253.6 40.4 %all-reduce = (f32[1024]{0:T(1024)}, f32[512]{0:T(512)}, f32[512]{0:T(512)}) all-reduce(f32[1024]{0:T(1024)S(1)} %get-tuple-element.14, f32[512]{0:T(512)S(1)} %get-tuple-element.16, f32[512]{0:T(512)S(1)} %bitcast.63), channel_id=1, replica_groups=mesh['dp'=4,'shard'=8] {'dp','shard'}, use_global_device_ids=true, to_apply=%region_4.5 | all-reduce | flops 2048 | bytes 16384 | tf_op jit(solution)/shard_map/psum | solution.py:69
  294.0 1.8 fusion.27
  295.8 23.6 %scatter_custom_fusion.1 = f32[2048,128]{1,0:T(8,128)} fusion(s32[4096]{0:T(1024)S(1)} %bitcast.61, f32[4096,128]{1,0:T(8,128)} %bitcast.64, f32[]{:T(128)} %constant.12.clone.1), kind=kCustom, calls=%fused_computation.28 | custom fusion | flops 524288 | bytes 1049088 | tf_op jit(solution)/shard_map/scatter-add | solution.py:67
  319.4 89.8 %all-reduce.4.cloned.1.call-done = (f32[1024,1024]{1,0:T(8,128)}, f32[1024,512]{1,0:T(8,128)}) async-done(((f32[1024,1024]{1,0:T(8,128)}, f32[1024,512]{1,0:T(8,128)}), (f32[1024,1024]{1,0:T(8,128)}, f32[1024,512]{1,0:T(8,128)})) %all-reduce.4.cloned.1.call-update) | async-done | bytes 6291472 | tf_op jit(solution)/shard_map/psum | solution.py:69
  409.2 4.9 %copy.49 = f32[1024,1024]{1,0:T(8,128)} copy(f32[1024,1024]{1,0:T(8,128)} %get-tuple-element.19) | data formatting | bytes 8388608
  414.1 0.0 copy-done.4
  414.1 1.3 copy.50
  (10 shorter events, 0.1 us)
Async XLA Ops:
  8.0 102.6 %copy-start = (bf16[1024,1024]{1,0:T(8,128)(2,1)S(1)}, bf16[1024,1024]{1,0:T(8,128)(2,1)}, u32[]{:S(2)}) copy-start(bf16[1024,1024]{1,0:T(8,128)(2,1)} %param.11) | copy-start | bytes 6291460
  8.0 13.9 %all-to-all-start = ((s32[8,1,128]{2,1,0:T(1,128)}), s32[8,1,128]{2,1,0:T(1,128)S(1)}, u32[]{:S(2)}, u32[]{:S(2)}) async-start(s32[8,1,128]{2,1,0:T(1,128)} %bitcast.62), calls=%async_computation | async-start | bytes 8192 | tf_op jit(solution)/shard_map/all_to_all | solution.py:24
  15.5 6.3 %copy-start.6 = (s32[512,8]{0,1:T(8,128)S(1)}, s32[512,8]{0,1:T(8,128)}, u32[]{:S(2)}) copy-start(s32[512,8]{0,1:T(8,128)} %param.18) | copy-start | bytes 49156
  15.5 6.5 %copy-start.1 = (f32[2048,128]{1,0:T(8,128)S(1)}, f32[2048,128]{1,0:T(8,128)}, u32[]{:S(2)}) copy-start(f32[2048,128]{1,0:T(8,128)} %param.10) | copy-start | bytes 3145732
  28.0 19.9 %all-to-all-start.1 = ((f32[8,128,128]{2,1,0:T(8,128)}), f32[8,128,128]{2,1,0:T(8,128)S(1)}, u32[]{:S(2)}, u32[]{:S(2)}) async-start(f32[8,128,128]{2,1,0:T(8,128)} %broadcast_select_fusion), calls=%async_computation.1 | async-start | bytes 1048576 | tf_op jit(solution)/shard_map/all_to_all | solution.py:25
  34.0 6.0 %copy-start.5 = (s32[512,8,4]{0,2,1:T(4,128)S(1)}, s32[512,8,4]{0,2,1:T(4,128)}, u32[]{:S(2)}) copy-start(s32[512,8,4]{0,2,1:T(4,128)} %param.17) | copy-start | bytes 196612
  34.0 261.8 %all-gather.3.cloned.1.call-start = ((), (), s32[]{:S(2)}) async-start(), calls=%async_computation.3 | async-start | bytes 2621440 | tf_op jit(solution)/shard_map/all_gather | solution.py:62
  102.7 7.9 %copy-start.8 = (f32[1024]{0:T(1024)S(1)}, f32[1024]{0:T(1024)}, u32[]{:S(2)}) copy-start(f32[1024]{0:T(1024)} %param.12) | copy-start | bytes 12292
  110.6 1.4 copy-start.7
  110.6 1.4 copy-start.9
  110.6 1.4 copy-start.10
  110.7 1.4 copy-start.11
  112.0 1.1 copy-start.14
  113.1 1.1 copy-start.12
  114.2 1.3 copy-start.2
  239.8 169.4 %all-reduce.4.cloned.1.call-start = ((), (), s32[]{:S(2)}) async-start(), calls=%async_computation.4 | async-start | bytes 12582912 | tf_op jit(solution)/shard_map/psum | solution.py:69
  239.8 4.0 copy-start.3
  247.2 5.6 %copy-start.13 = (f32[512,512]{1,0:T(8,128)S(1)}, f32[512,512]{1,0:T(8,128)}, u32[]{:S(2)}) copy-start(f32[512,512]{1,0:T(8,128)} %copy-done.12) | copy-start | bytes 3145732
  409.2 4.9 %copy-start.4 = (f32[1024,512]{1,0:T(8,128)S(1)}, f32[1024,512]{1,0:T(8,128)}, u32[]{:S(2)}) copy-start(f32[1024,512]{1,0:T(8,128)} %get-tuple-element.20) | copy-start | bytes 6291460
Sparse Core Ops, SparseCore 0:
  239.9 22.2 all-gather.2
Sparse Core Ops, SparseCore 1:
  247.3 161.9 all-reduce.3
where the time goes:
time: 424 us; the launch traced here: 423 us
  other arithmetic  133 us (31%)
  waiting for transfers between devices  92.5 us (22%)
  local copies, waits for them, and re-layouts  89 us (21%)
  blocking collectives  63.9 us (15%)
  between operations  15.8 us (4%)
  matrix products  14.7 us (3%)
  starting transfers between devices  13.7 us (3%)
    scatter-add x1, other arithmetic, on_device(): jnp.zeros(cache_flat.shape, jnp.float32).at[slots.reshape(-1)]  97.1 us
    psum x1, waiting for transfers between devices, on_device(): lax.psum((g_cross, g_top, g_cbias, g_tbias, g_out), ('dp', 'shard'))  89.8 us
    gather x1, local copies, waits for them, and re-layouts, on_device(): gathered = cache_flat[slots]  54.8 us
    psum x1, blocking collectives, on_device(): lax.psum((g_cross, g_top, g_cbias, g_tbias, g_out), ('dp', 'shard'))  40.4 us
    scatter-add x1, other arithmetic, on_device(): table_grad = jnp.zeros(table.shape, jnp.float32).at[every_ids.reshape(-1)...  23.6 us
    all_to_all x1, blocking collectives, on_device(): lax.all_to_all(slot_grads.reshape(cache.shape), 'shard', split_axis=0, co...  18 us
    unnamed x35, local copies, waits for them, and re-layouts  11.1 us
  transfers between devices with their start and end apart: 4, of which 2 were waited for; matrix products, arithmetic and copies ran while one was open for 12% of the time, Pallas kernels for 0%

commit v1 on v0

--- a/solution.py
+++ b/solution.py
@@ -66,7 +66,7 @@
         .at[every_ids.reshape(-1)]
         .add(every_grads.reshape(-1, emb))
     )
-    summed = lax.psum((g_cross, g_top, g_cbias, g_tbias, g_out), ("dp", "shard"))
+    summed = lax.psum(lax.psum((g_cross, g_top, g_cbias, g_tbias, g_out), "shard"), "dp")
     return (logits, summed[0], summed[1], summed[2], summed[3], summed[4], table_grad)
 
 

time: 424 us -> 469 us (1.11)
  waiting for transfers between devices: 92.5 us -> 145 us
  blocking collectives: 63.9 us -> 56.9 us
    psum x1 -> x2, waiting for transfers between devices: 89.8 us -> 134 us  [the longest x1 74.5 us: on_device(): lax.psum((g_cross, g_top, g_cbias, g_tbias, g_out), 'shard')]
    psum x1 -> x2, blocking collectives: 40.4 us -> 27.2 us  [the longest x1 19.6 us: on_device(): lax.psum((g_cross, g_top, g_cbias, g_tbias, g_out), 'shard')]
    all_to_all x1, blocking collectives: 18 us -> 24.4 us  [on_device(): lax.all_to_all(slot_grads.reshape(cache.shape), 'shard', split_axis=0, co...]
    all_to_all x1, waiting for transfers between devices: 0.01 us -> 5.57 us  [on_device(): lax.all_to_all(requests, 'shard', split_axis=0, concat_axis=0, tiled=True)]
    unnamed x35 -> x27, local copies, waits for them, and re-layouts: 11.1 us -> 12.3 us
  transfers between devices with their start and end apart: 4 -> 5, of which waited for: 2 -> 4; matrix products, arithmetic and copies ran while one was open for 12% -> 33% of each run, Pallas kernels for 0% -> 0%
where the time goes in v1:
time: 469 us; the launch traced here: 468 us
  waiting for transfers between devices  145 us (31%)
  other arithmetic  131 us (28%)
  local copies, waits for them, and re-layouts  90.1 us (19%)
  blocking collectives  56.9 us (12%)
  matrix products  17.3 us (4%)
  between operations  15.7 us (3%)
  starting transfers between devices  11.3 us (2%)
    scatter-add x1, other arithmetic, on_device(): jnp.zeros(cache_flat.shape, jnp.float32).at[slots.reshape(-1)]  96.2 us
    psum x1, waiting for transfers between devices, on_device(): lax.psum((g_cross, g_top, g_cbias, g_tbias, g_out), 'shard')  74.5 us
    psum x1, waiting for transfers between devices, on_device(): lax.psum(lax.psum((g_cross, g_top, g_cbias, g_tbias, g_out), 'shard'), 'dp')  60 us
    gather x1, local copies, waits for them, and re-layouts, on_device(): gathered = cache_flat[slots]  54.8 us
    all_to_all x1, blocking collectives, on_device(): lax.all_to_all(slot_grads.reshape(cache.shape), 'shard', split_axis=0, co...  24.4 us
    scatter-add x1, other arithmetic, on_device(): table_grad = jnp.zeros(table.shape, jnp.float32).at[every_ids.reshape(-1)...  23.6 us
    psum x1, blocking collectives, on_device(): lax.psum((g_cross, g_top, g_cbias, g_tbias, g_out), 'shard')  19.6 us
    unnamed x27, local copies, waits for them, and re-layouts  12.3 us
  transfers between devices with their start and end apart: 5, of which 4 were waited for; matrix products, arithmetic and copies ran while one was open for 33% of the time, Pallas kernels for 0%

profile of v1, /device:TPU:0, one launch (start us, length us, event | category | flops | bytes accessed | tf_op | source)
XLA Modules:
  0.0 468.2 jit_solution(11506217081057164717)
XLA Ops:
  8.0 0.0 copy-start
  8.0 7.5 %all-to-all-start = ((s32[8,1,128]{2,1,0:T(1,128)}), s32[8,1,128]{2,1,0:T(1,128)S(1)}, u32[]{:S(2)}, u32[]{:S(2)}) async-start(s32[8,1,128]{2,1,0:T(1,128)} %bitcast.62), calls=%async_computation | async-start | bytes 8192 | tf_op jit(solution)/shard_map/all_to_all | solution.py:24
  15.5 0.8 copy.25
  16.3 5.6 %all-to-all-done = s32[8,1,128]{2,1,0:T(1,128)S(1)} async-done(((s32[8,1,128]{2,1,0:T(1,128)}), s32[8,1,128]{2,1,0:T(1,128)S(1)}, u32[]{:S(2)}, u32[]{:S(2)}) %all-to-all-start) | async-done | bytes 4128 | tf_op jit(solution)/shard_map/all_to_all | solution.py:24
  21.9 4.0 gather_fusion
  25.9 0.0 copy-start.3
  26.0 1.0 broadcast_select_fusion
  26.9 3.5 all-to-all-start.1
  30.5 0.0 all-reduce.7.cloned.1.call-start
  30.5 0.0 copy-done.3
  30.5 2.0 copy.24
  32.5 3.2 reshape.160
  35.7 2.6 fusion.4
  38.3 5.4 %all-to-all-done.1 = f32[8,128,128]{2,1,0:T(8,128)S(1)} async-done(((f32[8,128,128]{2,1,0:T(8,128)}), f32[8,128,128]{2,1,0:T(8,128)S(1)}, u32[]{:S(2)}, u32[]{:S(2)}) %all-to-all-start.1) | async-done | bytes 524320 | tf_op jit(solution)/shard_map/all_to_all | solution.py:25
  43.7 54.8 %gather_fusion.1 = f32[16384,128]{1,0:T(8,128)} fusion(f32[1024,128]{1,0:T(8,128)S(1)} %bitcast.48, s32[16384]{0:T(1024)S(1)} %broadcast_clamp_fusion), kind=kCustom, calls=%fused_computation.1 | custom fusion | bytes 16842752 | tf_op jit(solution)/shard_map/gather | solution.py:32
  98.5 0.0 copy-start.5
  98.5 7.9 %multiply_reduce_fusion = bf16[512,8,128]{2,1,0:T(8,128)(2,1)S(1)} fusion(f32[512,8,4,128]{3,2,1,0:T(4,128)} %bitcast.49, f32[512,8,4]{2,1,0:T(8,128)} %fusion.4), kind=kLoop, calls=%fused_computation.6 | loop fusion | flops 3670016 | bytes 9502720 | tf_op jit(solution)/shard_map/reduce_sum | solution.py:33
  106.3 0.0 copy-done
  106.4 0.0 copy-done.5
  106.4 0.0 copy-start.4
  106.4 0.0 copy-start.6
  106.4 0.0 copy-start.7
  106.4 0.0 copy-start.8
  106.4 2.7 fusion.3
  109.1 0.0 copy-done.4
  109.1 0.0 copy-done.6
  109.1 0.0 copy-done.7
  109.1 0.0 copy-done.8
  109.1 1.0 fusion.33
  110.1 0.0 copy-start.9
  110.2 2.4 fusion.21
  112.5 0.0 copy-done.9
  112.5 1.1 fusion.5
  113.6 0.0 copy-start.1
  113.6 1.3 copy-done.1
  114.9 3.3 fusion.8
  118.3 0.0 all-reduce.7.cloned.1.call-update
  118.3 0.2 all-gather.3.cloned.1.call-start
  118.5 3.2 reshape.149
  121.7 2.0 copy.26
  123.7 3.3 reshape.146
  127.0 0.1 compare_select_fusion
  127.1 4.2 add_bitcast_fusion
  131.3 1.8 copy.28
  133.0 7.4 %mul.73 = f32[512,8,4,128]{3,2,1,0:T(4,128)} broadcast(f32[512,8,128]{2,1,0:T(8,128)} %bitcast.55), dimensions={0,1,3} | broadcast | bytes 10485760 | tf_op jit(solution)/shard_map/mul | solution.py:53
  140.4 96.2 %scatter_custom_fusion = f32[1024,128]{1,0:T(8,128)S(1)} fusion(s32[16384]{0:T(1024)S(1)} %bitcast.60, f32[16384,128]{1,0:T(8,128)} %bitcast.50, f32[16384]{0:T(1024)S(1)} %reshape.149, f32[]{:T(128)} %constant.12.clone.1), kind=kCustom, calls=%fused_computation.4 | custom fusion | flops 4194304 | bytes 8978436 | tf_op jit(solution)/shard_map/scatter-add | solution.py:55
  236.6 24.4 %all_to_all.25 = f32[8,128,128]{2,1,0:T(8,128)} all-to-all(f32[8,128,128]{2,1,0:T(8,128)S(1)} %bitcast.56), channel_id=1, replica_groups=mesh['dp'=4,'shard'=8] {'shard'}, dimensions={0} | all-to-all | bytes 1048576 | tf_op jit(solution)/shard_map/all_to_all | solution.py:57
  261.0 0.0 all-gather.3.cloned.1.call-update
  261.0 0.0 all-reduce.9.cloned.1.call-start
  261.1 74.5 %all-reduce.7.cloned.1.call-done = (f32[1024,1024]{1,0:T(8,128)}, f32[1024,512]{1,0:T(8,128)}) async-done(((f32[1024,1024]{1,0:T(8,128)}, f32[1024,512]{1,0:T(8,128)}), (f32[1024,1024]{1,0:T(8,128)}, f32[1024,512]{1,0:T(8,128)})) %all-reduce.7.cloned.1.call-update) | async-done | bytes 6291472 | tf_op jit(solution)/shard_map/psum | solution.py:69
  335.6 0.0 copy-start.10
  335.6 0.0 all-reduce.9.cloned.1.call-update
  335.6 5.3 %all-gather = s32[32,1,128]{2,1,0:T(1,128)S(1)} all-gather(s32[8,1,128]{2,1,0:T(1,128)S(1)} %all-to-all-done), channel_id=2, replica_groups=mesh['dp'=4,'shard'=8] {'dp'}, dimensions={0}, use_global_device_ids=true | all-gather | bytes 20480 | tf_op jit(solution)/shard_map/all_gather | solution.py:61
  341.0 0.0 copy-done.10
  341.0 0.9 fusion.25
  341.9 19.6 %all-reduce = (f32[1024]{0:T(1024)S(1)}, f32[512]{0:T(512)S(1)}, f32[512]{0:T(512)S(1)}) all-reduce(f32[1024]{0:T(1024)S(1)} %get-tuple-element.19, f32[512]{0:T(512)S(1)} %get-tuple-element.21, f32[512]{0:T(512)S(1)} %bitcast.63), channel_id=1, replica_groups=mesh['dp'=4,'shard'=8] {'shard'}, use_global_device_ids=true, to_apply=%region_6.7 | all-reduce | flops 2048 | bytes 16384 | tf_op jit(solution)/shard_map/psum | solution.py:69
  361.5 7.6 %all-reduce.2 = (f32[1024]{0:T(1024)}, f32[512]{0:T(512)}, f32[512]{0:T(512)}) all-reduce(f32[1024]{0:T(1024)S(1)} %get-tuple-element.7, f32[512]{0:T(512)S(1)} %get-tuple-element.8, f32[512]{0:T(512)S(1)} %get-tuple-element.9), channel_id=1, replica_groups=mesh['dp'=4,'shard'=8] {'dp'}, use_global_device_ids=true, to_apply=%region_7.8 | all-reduce | flops 2048 | bytes 16384 | tf_op jit(solution)/shard_map/psum | solution.py:69
  369.1 1.8 fusion.27
  370.9 0.0 all-gather.3.cloned.1.call-done
  370.9 23.6 %scatter_custom_fusion.1 = f32[2048,128]{1,0:T(8,128)} fusion(s32[4096]{0:T(1024)S(1)} %bitcast.61, f32[4096,128]{1,0:T(8,128)} %bitcast.64, f32[]{:T(128)} %constant.12.clone.1), kind=kCustom, calls=%fused_computation.28 | custom fusion | flops 524288 | bytes 1049088 | tf_op jit(solution)/shard_map/scatter-add | solution.py:67
  394.5 60.0 %all-reduce.9.cloned.1.call-done = (f32[1024,1024]{1,0:T(8,128)}, f32[1024,512]{1,0:T(8,128)}) async-done(((f32[1024,1024]{1,0:T(8,128)}, f32[1024,512]{1,0:T(8,128)}), (f32[1024,1024]{1,0:T(8,128)}, f32[1024,512]{1,0:T(8,128)})) %all-reduce.9.cloned.1.call-update) | async-done | bytes 6291472 | tf_op jit(solution)/shard_map/psum | solution.py:69
  454.5 4.9 %copy.51 = f32[1024,1024]{1,0:T(8,128)} copy(f32[1024,1024]{1,0:T(8,128)} %get-tuple-element.24) | data formatting | bytes 8388608
  459.4 0.0 copy-done.2
  459.4 1.3 copy.52
  (6 shorter events, 0.1 us)
Async XLA Ops:
  8.0 98.4 %copy-start = (bf16[1024,1024]{1,0:T(8,128)(2,1)S(1)}, bf16[1024,1024]{1,0:T(8,128)(2,1)}, u32[]{:S(2)}) copy-start(bf16[1024,1024]{1,0:T(8,128)(2,1)} %param.11) | copy-start | bytes 6291460
  8.0 13.9 %all-to-all-start = ((s32[8,1,128]{2,1,0:T(1,128)}), s32[8,1,128]{2,1,0:T(1,128)S(1)}, u32[]{:S(2)}, u32[]{:S(2)}) async-start(s32[8,1,128]{2,1,0:T(1,128)} %bitcast.62), calls=%async_computation | async-start | bytes 8192 | tf_op jit(solution)/shard_map/all_to_all | solution.py:24
  25.9 4.6 copy-start.3
  26.9 16.8 %all-to-all-start.1 = ((f32[8,128,128]{2,1,0:T(8,128)}), f32[8,128,128]{2,1,0:T(8,128)S(1)}, u32[]{:S(2)}, u32[]{:S(2)}) async-start(f32[8,128,128]{2,1,0:T(8,128)} %broadcast_select_fusion), calls=%async_computation.1 | async-start | bytes 1048576 | tf_op jit(solution)/shard_map/all_to_all | solution.py:25
  30.5 305.1 %all-reduce.7.cloned.1.call-start = ((), (), s32[]{:S(2)}) async-start(), calls=%async_computation.4 | async-start | bytes 12582912 | tf_op jit(solution)/shard_map/psum | solution.py:69
  98.5 7.9 %copy-start.5 = (f32[1024]{0:T(1024)S(1)}, f32[1024]{0:T(1024)}, u32[]{:S(2)}) copy-start(f32[1024]{0:T(1024)} %param.12) | copy-start | bytes 12292
  106.4 2.8 copy-start.4
  106.4 2.7 copy-start.6
  106.4 2.7 copy-start.7
  106.4 2.7 copy-start.8
  110.1 2.4 copy-start.9
  113.6 1.3 copy-start.1
  118.3 252.6 %all-gather.3.cloned.1.call-start = ((), (), s32[]{:S(2)}) async-start(), calls=%async_computation.3 | async-start | bytes 2621440 | tf_op jit(solution)/shard_map/all_gather | solution.py:62
  261.0 193.4 %all-reduce.9.cloned.1.call-start = ((), (), s32[]{:S(2)}) async-start(), calls=%async_computation.5 | async-start | bytes 12582912 | tf_op jit(solution)/shard_map/psum | solution.py:69
  335.6 5.4 %copy-start.10 = (f32[512,512]{1,0:T(8,128)S(1)}, f32[512,512]{1,0:T(8,128)}, u32[]{:S(2)}) copy-start(f32[512,512]{1,0:T(8,128)} %copy-done.9) | copy-start | bytes 3145732
  454.5 4.9 %copy-start.2 = (f32[1024,512]{1,0:T(8,128)S(1)}, f32[1024,512]{1,0:T(8,128)}, u32[]{:S(2)}) copy-start(f32[1024,512]{1,0:T(8,128)} %get-tuple-element.25) | copy-start | bytes 6291460
Sparse Core Ops, SparseCore 0:
  118.4 217.1 all-reduce.6
Sparse Core Ops, SparseCore 1:
  261.1 20.8 all-gather.2
  335.7 118.7 all-reduce.8
